TPU v7x, 128 devices: a whole 4x4x4 slice. The times are simulated.
128 devices in a mesh: song: 2 (over y_lo), seq: 64 (over z, x, y_hi, core).
Axes of the slice: x: 4, y: 4 (y_hi: 2, y_lo: 2; y = y_hi * 2 + y_lo), z: 4, core: 2. Of those that a mesh axis runs over, the one named last changes fastest.
Arguments:
- song_ids: int32 [16384], P(('song', 'seq')), parts along dimension 0, may hold values from 0 to 2047
- table: bfloat16 [2048, 2432], P(None, 'seq'), may hold values from -6 to 6
- position_table: bfloat16 [8192, 2432], P('seq'), may hold values from -4 to 4
- w_qkv: bfloat16 [2, 2432, 1800], replicated, may hold values from -4 to 4
- w_out: bfloat16 [2, 600, 2432], replicated, may hold values from -0.25 to 0.25
Outputs:
- stream_out: bfloat16 [16384, 2432], P(('song', 'seq')), parts along dimension 0
There are 2 independent parts, one for each index of `song`. A program takes and returns all parts, laid end to end along the dimension named above; an argument that names none is the same for every part. Nothing has to cross between parts.
All inputs are finite; a program needn't handle non-finite values.
Results may differ from a plain program's by a relative error of at most 0.0065.
Values may be sent and summed in bfloat16 or wider, within the bound.
No kernel may reach another device: no remote copies, remote signals or barrier semaphores. Data moves between devices by JAX's collectives and lax.ppermute only.
A program may use at most 192 MiB of HBM per device.

v0:
```python
import math
import jax
import jax.numpy as jnp
from jax import lax
from jax.sharding import PartitionSpec as P

HEADS = 4
HEAD = 150
epsilon = 1e-05


def from_behind(value, axis, by):
    length = lax.axis_size(axis)
    pairs = [(i, i + by) for i in range(length) if 0 <= i + by < length]
    return lax.ppermute(value, axis, pairs)


def normalize(residual):
    center_mean = jnp.mean(residual, axis=-1, keepdims=True)
    centered = residual - center_mean
    variance = jnp.mean(centered * centered, axis=-1, keepdims=True)
    return (centered * lax.rsqrt(variance + epsilon)).astype(jnp.bfloat16)


def project(residual, weight):
    joined = jnp.dot(normalize(residual), weight, preferred_element_type=jnp.float32).astype(
        jnp.bfloat16
    )
    return joined.reshape(residual.shape[0], HEADS, 3 * HEAD)


def softmax_rounded(scores):
    top_score = jnp.max(scores, axis=-1, keepdims=True)
    lifted = jnp.exp(scores - top_score)
    return (lifted / jnp.sum(lifted, axis=-1, keepdims=True)).astype(jnp.bfloat16)


def shards(song_ids, table, position_table, w_qkv, w_out):
    inv_root = 1.0 / math.sqrt(HEAD)
    axis_count = lax.axis_size("seq")
    row_index = lax.axis_index("seq")
    all_codes = lax.all_gather(song_ids, "seq", axis=0, tiled=True)
    picked = jnp.take(table, all_codes, axis=0)
    embedded = lax.all_to_all(picked, "seq", split_axis=0, concat_axis=1, tiled=True)
    residual = embedded.astype(jnp.float32) + position_table.astype(jnp.float32)
    local_tokens = residual.shape[0]
    joined = project(residual, w_qkv[0])
    every_row = lax.all_gather(joined[:, :, HEAD:], "seq", axis=0, tiled=True)
    row_grid = every_row.reshape(axis_count, local_tokens, HEADS, 2 * HEAD)
    scores = (
        jnp.einsum(
            "chd,rchd->chr",
            joined[:, :, :HEAD],
            row_grid[..., :HEAD],
            preferred_element_type=jnp.float32,
        )
        * inv_root
    )
    allowed = jnp.arange(axis_count) <= row_index
    probs = softmax_rounded(jnp.where(allowed, scores, -jnp.inf))
    mixed = jnp.einsum(
        "chr,rchd->chd", probs, row_grid[..., HEAD:], preferred_element_type=jnp.float32
    ).astype(jnp.bfloat16)
    residual = residual + jnp.dot(
        mixed.reshape(local_tokens, HEADS * HEAD), w_out[0], preferred_element_type=jnp.float32
    )
    joined = project(residual, w_qkv[1])
    before = from_behind(joined[:, :, HEAD:], "seq", 1)
    query = joined[:, :, :HEAD]
    far_scores = (
        jnp.einsum("chd,khd->hck", query, before[..., :HEAD], preferred_element_type=jnp.float32)
        * inv_root
    )
    far_scores = jnp.where(row_index > 0, far_scores, -jnp.inf)
    own_scores = (
        jnp.einsum(
            "chd,chd->hc", query, joined[:, :, HEAD : 2 * HEAD], preferred_element_type=jnp.float32
        )
        * inv_root
    )
    top_score = jnp.maximum(jnp.max(far_scores, axis=-1), own_scores)
    far_lifted = jnp.exp(far_scores - top_score[..., None])
    own_lifted = jnp.exp(own_scores - top_score)
    total = jnp.sum(far_lifted, axis=-1) + own_lifted
    far_probs = (far_lifted / total[..., None]).astype(jnp.bfloat16)
    own_probs = (own_lifted / total).astype(jnp.bfloat16)
    far_part = jnp.einsum(
        "hck,khd->chd", far_probs, before[..., HEAD:], preferred_element_type=jnp.float32
    )
    own_part = jnp.transpose(own_probs.astype(jnp.float32))[..., None] * joined[
        :, :, 2 * HEAD :
    ].astype(jnp.float32)
    mixed = (far_part + own_part).astype(jnp.bfloat16)
    residual = residual + jnp.dot(
        mixed.reshape(local_tokens, HEADS * HEAD), w_out[1], preferred_element_type=jnp.float32
    )
    return residual.astype(jnp.bfloat16)


def solution(mesh):
    in_specs = (P(("song", "seq")), P(None, "seq"), P("seq", None), P(), P())
    out_specs = P(("song", "seq"), None)
    return jax.shard_map(shards, mesh=mesh, in_specs=in_specs, out_specs=out_specs, check_vma=False)
```

profile of v0, /device:TPU:32, one launch (start us, length us, event | category | flops | bytes accessed | tf_op | source)
XLA Modules:
  0.0 349.5 jit_solution(981527527557596328)
XLA Ops:
  6.5 83.1 %all-gather = s32[64,1,128]{2,1,0:T(1,128)S(1)} all-gather(s32[1,1,128]{2,1,0:T(1,128)} %bitcast.80), channel_id=1, replica_groups=mesh['song'=2,'seq'=64] {'seq'}, dimensions={0}, use_global_device_ids=true | all-gather | bytes 33280 | tf_op jit(solution)/shard_map/all_gather | solution.py:42
  89.7 1.2 copy.17
  90.9 24.0 %gather_fusion = bf16[8192,38]{1,0:T(8,128)(2,1)S(1)} fusion(bf16[2048,38]{1,0:T(8,128)(2,1)S(1)} %copy.17, s32[8192]{0:T(1024)S(1)} %fusion.43), kind=kCustom, calls=%fused_computation | custom fusion | bytes 1277952 | tf_op jit(solution)/shard_map/jit(_take)/gather | solution.py:43
  115.0 1.0 copy.18
  116.0 0.1 broadcast_select_fusion
  116.1 31.4 %all_to_all.10 = bf16[64,128,38]{1,2,0:T(8,128)(2,1)S(1)} all-to-all(bf16[64,128,38]{1,2,0:T(8,128)(2,1)S(1)} %broadcast_select_fusion), channel_id=1, replica_groups=mesh['song'=2,'seq'=64] {'seq'}, dimensions={0} | all-to-all | bytes 1245184 | tf_op jit(solution)/shard_map/all_to_all | solution.py:44
  147.5 0.1 convert_bitcast_fusion
  147.6 0.1 reshape.65
  147.7 0.4 copy.19
  148.1 0.7 copy-done
  148.7 0.2 fusion.39
  149.0 0.3 multiply_reduce_fusion.3
  149.3 6.2 %fusion.13 = bf16[128,1800]{0,1:T(8,128)(2,1)S(1)} fusion(bf16[2,2432,1800]{1,2,0:T(8,128)(2,1)} %param.8, f32[128]{0:T(128)S(1)} %add_rsqrt_fusion.1, f32[128]{0:T(128)S(1)} %broadcast_multiply_fusion.1, f32[128,2432]{1,0:T(8,128)S(1)} %copy.19, bf16[128,2432]{1,0:T(8,128)(2,1)S(1)} %copy-done), kind=kOutput, calls=%fused_computation.20 | convolution fusion | flops 1122452480 | bytes 11084800 | tf_op jit(solution)/shard_map/dot_general | solution.py:26
  155.5 0.1 reshape.60
  155.6 0.8 slice.59
  156.5 117.3 %all-gather.3.cloned.1.call-done = bf16[8192,4,300]{0,2,1:T(8,128)(2,1)} async-done(((bf16[128,4,300]{0,2,1:T(8,128)(2,1)}), bf16[8192,4,300]{0,2,1:T(8,128)(2,1)}) %all-gather.3.cloned.1.call-update) | async-done | bytes 19660816 | tf_op jit(solution)/shard_map/all_gather | solution.py:48
  273.8 27.6 %reshape.61 = bf16[64,128,4,300]{1,0,3,2:T(8,128)(2,1)} reshape(bf16[8192,4,300]{0,2,1:T(8,128)(2,1)} %all-gather.3.cloned.1.call-done) | data formatting | bytes 39321600 | tf_op jit(solution)/shard_map/reshape | solution.py:49
  301.3 6.7 %multiply_reduce_fusion.1 = f32[128,4,64]{0,2,1:T(8,128)S(1)} fusion(bf16[64,128,4,300]{1,0,3,2:T(8,128)(2,1)} %reshape.61, f32[128,4,150]{0,2,1:T(8,128)S(1)} %slice_convert_fusion), kind=kLoop, calls=%fused_computation.4 | loop fusion | flops 14712832 | bytes 10268672 | tf_op jit(solution)/shard_map/chd,rchd->chr/dot_general | solution.py:51
  308.0 0.1 fusion.26
  308.2 8.3 %multiply_reduce_fusion = bf16[128,4,150]{0,2,1:T(8,128)(2,1)S(1)} fusion(bf16[64,128,4,300]{1,0,3,2:T(8,128)(2,1)} %reshape.61, f32[128,4,64]{0,2,1:T(8,128)S(1)} %fusion.26), kind=kLoop, calls=%fused_computation.3 | loop fusion | flops 14668800 | bytes 10115072 | tf_op jit(solution)/shard_map/chr,rchd->chd/dot_general | solution.py:61
  316.6 2.6 fusion.53
  319.2 0.3 multiply_reduce_fusion.2
  319.5 6.2 %fusion.16 = bf16[128,1800]{0,1:T(8,128)(2,1)S(1)} fusion(bf16[2,2432,1800]{1,2,0:T(8,128)(2,1)} %param.8, f32[128,2432]{1,0:T(8,128)S(1)} %get-tuple-element.6, f32[128]{0:T(128)S(1)} %add_rsqrt_fusion, f32[128]{0:T(128)S(1)} %broadcast_multiply_fusion), kind=kOutput, calls=%fused_computation.21 | convolution fusion | flops 1121829888 | bytes 10462208 | tf_op jit(solution)/shard_map/dot_general | solution.py:26
  325.7 0.1 reshape.63
  325.8 0.1 slice.62
  325.9 2.2 collective-permute-start
  328.1 0.1 fusion.31
  328.1 10.5 %collective-permute-done = bf16[128,4,300]{0,2,1:T(8,128)(2,1)S(1)} collective-permute-done((bf16[128,4,300]{0,2,1:T(8,128)(2,1)S(1)}, bf16[128,4,300]{0,2,1:T(8,128)(2,1)S(1)}, u32[]{:S(2)}, u32[]{:S(2)}) %collective-permute-start) | collective-permute-done | bytes 307232 | tf_op jit(solution)/shard_map/ppermute | solution.py:15
  338.6 0.3 fusion.54
  338.9 0.1 fusion.32
  339.0 0.3 fusion.21
  339.3 3.4 fusion.8
  (16 shorter events, 0.2 us)
Async XLA Ops:
  6.5 267.2 %all-gather.3.cloned.1.call-start = ((), (), s32[]{:S(2)}) async-start(), calls=%async_computation.1 | async-start | bytes 20234240 | tf_op jit(solution)/shard_map/all_gather | solution.py:48
  147.7 1.1 copy-start
  325.9 12.7 %collective-permute-start = (bf16[128,4,300]{0,2,1:T(8,128)(2,1)S(1)}, bf16[128,4,300]{0,2,1:T(8,128)(2,1)S(1)}, u32[]{:S(2)}, u32[]{:S(2)}) collective-permute-start(bf16[128,4,300]{0,2,1:T(8,128)(2,1)S(1)} %slice.62), channel_id=1, source_target_pairs={{0,1},{1,2},{2,3},{3,4},{4,5},{5,6},{6,7},{7,8},{8,9},{9,10},{10,1... | collective-permute-start | bytes 921608 | tf_op jit(solution)/shard_map/ppermute | solution.py:15
Sparse Core Ops, SparseCore 0:
  156.5 117.1 all-gather.2
where the time goes:
time: 350 us
  waiting for transfers between devices  128 us (37%)
  blocking collectives  115 us (33%)
  local copies, waits for them, and re-layouts  56.2 us (16%)
  matrix products  18.9 us (5%)
  other arithmetic  16.4 us (5%)
  between operations  13.6 us (4%)
    all_gather x1, waiting for transfers between devices, shards(): every_row = lax.all_gather(joined[:, :, HEAD:], 'seq', axis=0, tiled=True)  117 us
    all_gather x1, blocking collectives, shards(): all_codes = lax.all_gather(song_ids, 'seq', axis=0, tiled=True)  83.1 us
    all_to_all x1, blocking collectives, shards(): lax.all_to_all(picked, 'seq', split_axis=0, concat_axis=1, tiled=True)  31.4 us
    reshape x1, local copies, waits for them, and re-layouts, shards(): row_grid = every_row.reshape(axis_count, local_tokens, HEADS, 2 * HEAD)  27.6 us
    gather x2, local copies, waits for them, and re-layouts, shards(): picked = jnp.take(table, all_codes, axis=0)  25 us
    dot_general x2, matrix products, project(): jnp.dot(normalize(residual), weight, preferred_element_type=jnp.float32)  12.3 us
    ppermute x1, waiting for transfers between devices, from_behind(): return lax.ppermute(value, axis, pairs)  10.5 us
    dot_general x1, other arithmetic, shards(): jnp.einsum('chr,rchd->chd', probs, row_grid[..., HEAD:], preferred_elemen...  8.34 us
  transfers between devices with their start and end apart: 2, of which 2 were waited for; matrix products, arithmetic and copies ran while one was open for 0% of the time, Pallas kernels for 0%

commit v1 on v0

--- a/solution.py
+++ b/solution.py
@@ -41,7 +41,16 @@
     row_index = lax.axis_index("seq")
     all_codes = lax.all_gather(song_ids, "seq", axis=0, tiled=True)
     picked = jnp.take(table, all_codes, axis=0)
-    embedded = lax.all_to_all(picked, "seq", split_axis=0, concat_axis=1, tiled=True)
+    begin_the_racks = lambda x_in, in_dim, dim_at: jnp.concatenate(
+        jax.lax.all_to_all(
+            jnp.stack(jnp.split(x_in, jax.lax.axis_size("seq"), axis=in_dim), axis=0),
+            axis_name="seq",
+            concat_axis=0,
+            split_axis=0,
+        ),
+        axis=dim_at,
+    )
+    embedded = begin_the_racks(picked, 0, 1)
     residual = embedded.astype(jnp.float32) + position_table.astype(jnp.float32)
     local_tokens = residual.shape[0]
     joined = project(residual, w_qkv[0])

time: 350 us -> 355 us (1.014)
  other arithmetic: 16.4 us -> 20.6 us
    select_n x1, other arithmetic: 0.08 us -> 4.27 us  [shards(): picked = jnp.take(table, all_codes, axis=0)]
    gather x2 -> x1, local copies, waits for them, and re-layouts: 25 us -> 24 us  [shards(): picked = jnp.take(table, all_codes, axis=0)]
where the time goes in v1:
time: 355 us
  waiting for transfers between devices  128 us (36%)
  blocking collectives  115 us (32%)
  local copies, waits for them, and re-layouts  56.8 us (16%)
  other arithmetic  20.6 us (6%)
  matrix products  18.9 us (5%)
  between operations  13.9 us (4%)
    all_gather x1, waiting for transfers between devices, shards(): every_row = lax.all_gather(joined[:, :, HEAD:], 'seq', axis=0, tiled=True)  117 us
    all_gather x1, blocking collectives, shards(): all_codes = lax.all_gather(song_ids, 'seq', axis=0, tiled=True)  83.1 us
    all_to_all x1, blocking collectives, shards(): jax.lax.all_to_all(jnp.stack(jnp.split(x_in, jax.lax.axis_size('seq'), ax...  31.4 us
    reshape x1, local copies, waits for them, and re-layouts, shards(): row_grid = every_row.reshape(axis_count, local_tokens, HEADS, 2 * HEAD)  27.6 us
    gather x1, local copies, waits for them, and re-layouts, shards(): picked = jnp.take(table, all_codes, axis=0)  24 us
    dot_general x2, matrix products, project(): jnp.dot(normalize(residual), weight, preferred_element_type=jnp.float32)  12.3 us
    ppermute x1, waiting for transfers between devices, from_behind(): return lax.ppermute(value, axis, pairs)  10.5 us
    dot_general x1, other arithmetic, shards(): jnp.einsum('chr,rchd->chd', probs, row_grid[..., HEAD:], preferred_elemen...  8.34 us
  transfers between devices with their start and end apart: 2, of which 2 were waited for; matrix products, arithmetic and copies ran while one was open for 0% of the time, Pallas kernels for 0%

profile of v1, /device:TPU:32, one launch (start us, length us, event | category | flops | bytes accessed | tf_op | source)
XLA Modules:
  0.0 354.6 jit_solution(16140259333840494726)
XLA Ops:
  6.5 83.1 %all-gather = s32[64,1,128]{2,1,0:T(1,128)S(1)} all-gather(s32[1,1,128]{2,1,0:T(1,128)} %bitcast.332), channel_id=1, replica_groups=mesh['song'=2,'seq'=64] {'seq'}, dimensions={0}, use_global_device_ids=true | all-gather | bytes 33280 | tf_op jit(solution)/shard_map/all_gather | solution.py:42
  89.7 1.2 copy.81
  90.9 24.0 %gather_fusion = bf16[8192,38]{1,0:T(8,128)(2,1)S(1)} fusion(bf16[2048,38]{1,0:T(8,128)(2,1)S(1)} %copy.81, s32[8192]{0:T(1024)S(1)} %fusion.43), kind=kCustom, calls=%fused_computation | custom fusion | bytes 1277952 | tf_op jit(solution)/shard_map/jit(_take)/gather | solution.py:43
  115.0 4.3 %broadcast_select_fusion = bf16[8192,38]{1,0:T(8,128)(2,1)S(1)} fusion(bf16[8192,38]{1,0:T(8,128)(2,1)S(1)} %gather_fusion, pred[8192]{0:T(1024)(128)(4,1)S(1)} %compare_and_fusion), kind=kLoop, calls=%fused_computation.22 | loop fusion | flops 311296 | bytes 1253376 | tf_op jit(solution)/shard_map/jit(_take)/select_n | solution.py:43
  120.2 1.0 copy.82
  121.3 31.4 %all_to_all.5 = bf16[64,128,38]{1,2,0:T(8,128)(2,1)S(1)} all-to-all(bf16[64,128,38]{1,2,0:T(8,128)(2,1)S(1)} %copy.82), channel_id=1, replica_groups=mesh['song'=2,'seq'=64] {'seq'}, dimensions={0} | all-to-all | bytes 1245184 | tf_op jit(solution)/shard_map/all_to_all | solution.py:45
  152.6 0.1 convert_bitcast_fusion
  152.7 0.1 reshape.58
  152.8 0.4 copy.83
  153.2 0.6 copy-done
  153.8 0.2 fusion.39
  154.0 0.3 multiply_reduce_fusion.3
  154.3 6.2 %fusion.13 = bf16[128,1800]{0,1:T(8,128)(2,1)S(1)} fusion(bf16[2,2432,1800]{1,2,0:T(8,128)(2,1)} %param.8, f32[128]{0:T(128)S(1)} %add_rsqrt_fusion.1, f32[128]{0:T(128)S(1)} %broadcast_multiply_fusion.1, f32[128,2432]{1,0:T(8,128)S(1)} %copy.83, bf16[128,2432]{1,0:T(8,128)(2,1)S(1)} %copy-done), kind=kOutput, calls=%fused_computation.20 | convolution fusion | flops 1122452480 | bytes 11084800 | tf_op jit(solution)/shard_map/dot_general | solution.py:26
  160.5 0.1 reshape.53
  160.7 0.8 slice.59
  161.5 117.3 %all-gather.3.cloned.1.call-done = bf16[8192,4,300]{0,2,1:T(8,128)(2,1)} async-done(((bf16[128,4,300]{0,2,1:T(8,128)(2,1)}), bf16[8192,4,300]{0,2,1:T(8,128)(2,1)}) %all-gather.3.cloned.1.call-update) | async-done | bytes 19660816 | tf_op jit(solution)/shard_map/all_gather | solution.py:57
  278.8 27.6 %reshape.54 = bf16[64,128,4,300]{1,0,3,2:T(8,128)(2,1)} reshape(bf16[8192,4,300]{0,2,1:T(8,128)(2,1)} %all-gather.3.cloned.1.call-done) | data formatting | bytes 39321600 | tf_op jit(solution)/shard_map/reshape | solution.py:58
  306.4 6.7 %multiply_reduce_fusion.1 = f32[128,4,64]{0,2,1:T(8,128)S(1)} fusion(bf16[64,128,4,300]{1,0,3,2:T(8,128)(2,1)} %reshape.54, f32[128,4,150]{0,2,1:T(8,128)S(1)} %slice_convert_fusion), kind=kLoop, calls=%fused_computation.4 | loop fusion | flops 14712832 | bytes 10268672 | tf_op jit(solution)/shard_map/chd,rchd->chr/dot_general | solution.py:60
  313.1 0.1 fusion.26
  313.2 8.3 %multiply_reduce_fusion = bf16[128,4,150]{0,2,1:T(8,128)(2,1)S(1)} fusion(bf16[64,128,4,300]{1,0,3,2:T(8,128)(2,1)} %reshape.54, f32[128,4,64]{0,2,1:T(8,128)S(1)} %fusion.26), kind=kLoop, calls=%fused_computation.3 | loop fusion | flops 14668800 | bytes 10115072 | tf_op jit(solution)/shard_map/chr,rchd->chd/dot_general | solution.py:70
  321.6 2.6 fusion.53
  324.3 0.3 multiply_reduce_fusion.2
  324.5 6.2 %fusion.16 = bf16[128,1800]{0,1:T(8,128)(2,1)S(1)} fusion(bf16[2,2432,1800]{1,2,0:T(8,128)(2,1)} %param.8, f32[128,2432]{1,0:T(8,128)S(1)} %get-tuple-element.6, f32[128]{0:T(128)S(1)} %add_rsqrt_fusion, f32[128]{0:T(128)S(1)} %broadcast_multiply_fusion), kind=kOutput, calls=%fused_computation.21 | convolution fusion | flops 1121829888 | bytes 10462208 | tf_op jit(solution)/shard_map/dot_general | solution.py:26
  330.7 0.1 reshape.56
  330.9 0.1 slice.62
  330.9 2.2 collective-permute-start
  333.1 0.1 fusion.31
  333.2 10.5 %collective-permute-done = bf16[128,4,300]{0,2,1:T(8,128)(2,1)S(1)} collective-permute-done((bf16[128,4,300]{0,2,1:T(8,128)(2,1)S(1)}, bf16[128,4,300]{0,2,1:T(8,128)(2,1)S(1)}, u32[]{:S(2)}, u32[]{:S(2)}) %collective-permute-start) | collective-permute-done | bytes 307232 | tf_op jit(solution)/shard_map/ppermute | solution.py:15
  343.7 0.3 fusion.54
  344.0 0.1 fusion.32
  344.1 0.3 fusion.21
  344.4 3.4 fusion.8
  (80 shorter events, 0.9 us)
Async XLA Ops:
  6.5 272.3 %all-gather.3.cloned.1.call-start = ((), (), s32[]{:S(2)}) async-start(), calls=%async_computation.1 | async-start | bytes 20234240 | tf_op jit(solution)/shard_map/all_gather | solution.py:57
  152.7 1.1 copy-start
  330.9 12.7 %collective-permute-start = (bf16[128,4,300]{0,2,1:T(8,128)(2,1)S(1)}, bf16[128,4,300]{0,2,1:T(8,128)(2,1)S(1)}, u32[]{:S(2)}, u32[]{:S(2)}) collective-permute-start(bf16[128,4,300]{0,2,1:T(8,128)(2,1)S(1)} %slice.62), channel_id=1, source_target_pairs={{0,1},{1,2},{2,3},{3,4},{4,5},{5,6},{6,7},{7,8},{8,9},{9,10},{10,1... | collective-permute-start | bytes 921608 | tf_op jit(solution)/shard_map/ppermute | solution.py:15
Sparse Core Ops, SparseCore 0:
  161.6 117.1 all-gather.2
